TPU v7x, 32 devices: a whole 2x2x4 slice. The times are simulated.
32 devices in a mesh: space: 4 (over y, core), shard: 8 (over z, x).
Axes of the slice: x: 2, y: 2, z: 4, core: 2. Of those that a mesh axis runs over, the one named last changes fastest.
Arguments:
- volume_field: float32 [2, 16, 16, 128, 128], P(None, None, 'space', 'shard'), may hold values from -6 to 6
- source: float32 [2, 16, 16, 128, 128], P(None, None, 'space', 'shard'), may hold values from -6 to 6
- material: int32 [16, 128, 128], P('space', 'shard'), may hold values from 0 to 7
- mat_real: float32 [8], replicated, may hold values from 0.5 to 4
- mat_loss: float32 [8], replicated, may hold values from 0.1 to 1.5
- surface_map: int32 [512, 128], P(('space', 'shard')), may hold values from 0 to 8191
- near_boxes: int32 [512, 4], P(('space', 'shard')), may hold values from 0 to 511, as said below
- near_blocks: bfloat16 [4, 256, 256], replicated, may hold values from -0.1875 to 0.1875
- radiate: bfloat16 [2, 128, 512], replicated, may hold values from -0.375 to 0.375
- interp: bfloat16 [512, 2048], replicated, may hold values from -0.25 to 0.25
- phase_angle: float32 [8, 2048], replicated, may hold values from -3.140625 to 3.140625
- far_parents: int32 [64, 8], replicated, may hold values from 0 to 63
- far_kind: int32 [64, 8], replicated, may hold values from 0 to 315
- translate: float32 [316, 2, 2048], P(None, None, 'shard'), may hold values from -0.18 to 0.18
Outputs:
- volume_out: float32 [2, 16, 16, 128, 128], P(None, None, 'space', 'shard')
- forcing: float32 [512, 16, 256], P(('space', 'shard'))
Inputs may be any that keep to these rules, and one draw needn't show every extreme that they name: near_boxes[b, 0] = b; every other entry is a box of the same group of 128 boxes (boxes g * 128 to (g + 1) * 128 - 1) whose index lies from 16 below to 31 above the first box of b's run of 16 boxes.
All inputs are finite; a program needn't handle non-finite values.
Results may differ from a plain program's by a relative error of at most 0.015.
Values may be sent and summed in bfloat16 or wider, within the bound.
No kernel may reach another device: no remote copies, remote signals or barrier semaphores. Data moves between devices by JAX's collectives and lax.ppermute only.
A program may use at most 128 MiB of HBM per device.

v0:
```python
import math
import jax
import jax.numpy as jnp
from jax import lax
from jax.sharding import PartitionSpec as P

relaxation = 0.8


def padded_2(array, sides, width):
    for axis, dim in sides:
        peers, length = (lax.axis_size(axis), array.shape[dim])
        up = [(i, (i + 1) % peers) for i in range(peers - 1)]
        down = [(j, i) for i, j in up]
        last = lax.slice_in_dim(array, length - width, length, axis=dim)
        leading = lax.slice_in_dim(array, 0, width, axis=dim)
        before = lax.ppermute(last, axis, up)
        after = lax.ppermute(leading, axis, down)
        array = jnp.concatenate([before, array, after], axis=dim)
    return array


def neighbour_sum(padded):
    core = padded[:, :, 1:-1, 1:-1]
    result = padded[:, :, 2:, 1:-1] + padded[:, :, :-2, 1:-1]
    result = result + padded[:, :, 1:-1, 2:] + padded[:, :, 1:-1, :-2]
    zero_layer = jnp.zeros(core.shape[:-1] + (1,), core.dtype)
    upper = jnp.concatenate([core[..., 1:], zero_layer], axis=-1)
    lower = jnp.concatenate([zero_layer, core[..., :-1]], axis=-1)
    return result + upper + lower


def relax_sweep(current, neighbours, source, diagonal_coef, loss_coef):
    real_part = diagonal_coef * current[0] - neighbours[0] - loss_coef * current[1]
    imag_part = diagonal_coef * current[1] - neighbours[1] + loss_coef * current[0]
    applied = jnp.stack([real_part, imag_part])
    return current + relaxation * (source - applied) / diagonal_coef


def block_matrix(radiate):
    upper = jnp.concatenate([radiate[0], radiate[1]], axis=1)
    lower = jnp.concatenate([-radiate[1], radiate[0]], axis=1)
    return jnp.concatenate([upper, lower], axis=0)


def aggregate(leaf_rows, interp, cosine, sine_part):
    parent_count = leaf_rows.shape[0] // 8
    excite = leaf_rows.shape[1]
    spread = jnp.dot(
        leaf_rows.reshape(-1, interp.shape[0]), interp, preferred_element_type=jnp.float32
    )
    spread = spread.reshape(parent_count, 8, excite, 2, interp.shape[1])
    cosine_wide = cosine[None, :, None, :]
    sine_wide = sine_part[None, :, None, :]
    real_part = jnp.sum(cosine_wide * spread[:, :, :, 0] - sine_wide * spread[:, :, :, 1], axis=1)
    imag_part = jnp.sum(sine_wide * spread[:, :, :, 0] + cosine_wide * spread[:, :, :, 1], axis=1)
    return jnp.stack([real_part, imag_part], axis=2).astype(jnp.bfloat16)


def combine_far(sources, table):
    real_table = table[:, :, None, 0]
    imag_table = table[:, :, None, 1]
    real_part = jnp.sum(real_table * sources[:, :, :, 0] - imag_table * sources[:, :, :, 1], axis=1)
    imag_part = jnp.sum(imag_table * sources[:, :, :, 0] + real_table * sources[:, :, :, 1], axis=1)
    return jnp.stack([real_part, imag_part], axis=2)


def disaggregate(incoming_rows, interp, cosine, sine_part, weights):
    parent_count = incoming_rows.shape[0]
    excite = incoming_rows.shape[1]
    widened = incoming_rows.astype(jnp.float32)[:, None]
    cosine_wide = cosine[None, :, None, :]
    sine_wide = sine_part[None, :, None, :]
    real_part = cosine_wide * widened[:, :, :, 0] + sine_wide * widened[:, :, :, 1]
    imag_part = cosine_wide * widened[:, :, :, 1] - sine_wide * widened[:, :, :, 0]
    shifted = jnp.stack([real_part, imag_part], axis=3).astype(jnp.bfloat16)
    leaf_in = jnp.dot(
        shifted.reshape(-1, interp.shape[1]), interp.T, preferred_element_type=jnp.float32
    ).astype(jnp.bfloat16)
    leaf_in = leaf_in.reshape(parent_count * 8 * excite, 2 * interp.shape[0])
    far_part = jnp.dot(leaf_in, weights.T, preferred_element_type=jnp.float32)
    return far_part.reshape(parent_count * 8, excite, weights.shape[0])


def select_cells(flat_field, cell_keys):
    cell_total = flat_field.shape[1]
    block_cells = math.gcd(cell_total, 1024)
    block_total = cell_total // block_cells
    positions = jnp.arange(block_cells, dtype=jnp.int32)

    def add_block(block_index, total):
        first = block_index * block_cells
        piece = lax.dynamic_slice_in_dim(flat_field, first, block_cells, 1)
        selector = (cell_keys[None, :] == (first + positions)[:, None]).astype(jnp.bfloat16)
        return total + jnp.dot(piece, selector, preferred_element_type=jnp.float32)

    empty = jnp.zeros((flat_field.shape[0], cell_keys.shape[0]), jnp.float32)
    return lax.fori_loop(0, block_total, add_block, empty)


def shards(
    volume_field,
    source,
    material,
    mat_real,
    mat_loss,
    surface_map,
    near_boxes,
    near_blocks,
    radiate,
    interp,
    phase_angle,
    far_parents,
    far_kind,
    translate,
):
    excite = volume_field.shape[1]
    cells_x = volume_field.shape[2]
    cells_y = volume_field.shape[3]
    cells_z = volume_field.shape[4]
    diagonal_coef = jnp.full(material.shape, 6.0, jnp.float32)
    loss_coef = jnp.zeros(material.shape, jnp.float32)
    for material_kind in range(mat_real.shape[0]):
        present = material == material_kind
        diagonal_coef = diagonal_coef + jnp.where(present, mat_real[material_kind], 0.0)
        loss_coef = loss_coef + jnp.where(present, mat_loss[material_kind], 0.0)
    channels = 2 * excite
    stacked = jnp.concatenate(
        [
            volume_field.reshape(channels, cells_x, cells_y, cells_z),
            source.reshape(channels, cells_x, cells_y, cells_z),
            diagonal_coef[None],
            loss_coef[None],
        ],
        axis=0,
    )
    widened = padded_2(stacked.astype(jnp.bfloat16), (("space", 1), ("shard", 2)), 2).astype(
        stacked.dtype
    )
    outer_field = widened[:channels].reshape(2, excite, cells_x + 4, cells_y + 4, cells_z)
    outer_source = widened[channels : 2 * channels, 1:-1, 1:-1].reshape(
        2, excite, cells_x + 2, cells_y + 2, cells_z
    )
    row_global = lax.axis_index("space") * cells_x - 1 + jnp.arange(cells_x + 2, dtype=jnp.int32)
    column_global = lax.axis_index("shard") * cells_y - 1 + jnp.arange(cells_y + 2, dtype=jnp.int32)
    row_inside = (row_global >= 0) & (row_global < cells_x * lax.axis_size("space"))
    column_inside = (column_global >= 0) & (column_global < cells_y * lax.axis_size("shard"))
    inside = row_inside[:, None, None] & column_inside[None, :, None]
    outer_diagonal = jnp.where(inside, widened[2 * channels, 1:-1, 1:-1], 1.0)
    outer_loss = widened[2 * channels + 1, 1:-1, 1:-1]
    first_sweep = relax_sweep(
        outer_field[:, :, 1:-1, 1:-1],
        neighbour_sum(outer_field),
        outer_source,
        outer_diagonal,
        outer_loss,
    )
    first_sweep = jnp.where(inside, first_sweep, 0.0)
    current = relax_sweep(
        first_sweep[:, :, 1:-1, 1:-1], neighbour_sum(first_sweep), source, diagonal_coef, loss_coef
    )
    box_count = surface_map.shape[0]
    unknowns = surface_map.shape[1]
    flat_field = current.reshape(2 * excite, cells_x * cells_y * cells_z).astype(jnp.bfloat16)
    sampled = select_cells(flat_field, surface_map.reshape(-1)).astype(jnp.bfloat16)
    sampled = sampled.reshape(2, excite, box_count, unknowns)
    currents = jnp.transpose(sampled, (2, 1, 0, 3)).reshape(box_count, excite, 2 * unknowns)
    device_rank = lax.axis_index("space") * lax.axis_size("shard") + lax.axis_index("shard")
    beside_all = padded_2(currents, (("shard", 0),), box_count)
    local_near = near_boxes - (device_rank * box_count - box_count)
    near_force = jnp.zeros((box_count, excite, 2 * unknowns), jnp.float32)
    for slot_index in range(near_boxes.shape[1]):
        picked = jnp.take(beside_all, local_near[:, slot_index], axis=0).reshape(
            box_count * excite, 2 * unknowns
        )
        near_force = near_force + jnp.dot(
            picked, near_blocks[slot_index], preferred_element_type=jnp.float32
        ).reshape(box_count, excite, 2 * unknowns)
    weights = block_matrix(radiate)
    leaf_dirs = interp.shape[0]
    leaf = jnp.dot(
        currents.reshape(box_count * excite, 2 * unknowns),
        weights,
        preferred_element_type=jnp.float32,
    ).astype(jnp.bfloat16)
    leaf = leaf.reshape(box_count, excite, 2, leaf_dirs)
    cosine = jnp.cos(phase_angle)
    sine_part = jnp.sin(phase_angle)
    parent_patterns = aggregate(leaf, interp, cosine, sine_part)
    directed = lax.all_to_all(parent_patterns, "shard", split_axis=3, concat_axis=0, tiled=True)
    group_parents = directed.shape[0]
    group_index = lax.axis_index("space")
    target_ids = lax.dynamic_slice_in_dim(
        far_parents, group_index * group_parents, group_parents, 0
    )
    target_kinds = lax.dynamic_slice_in_dim(far_kind, group_index * group_parents, group_parents, 0)
    table = jnp.take(translate, target_kinds, axis=0)
    gathered = lax.all_gather(directed, "space", axis=0, tiled=True)
    sources = jnp.take(gathered, target_ids, axis=0).astype(jnp.float32)
    incoming = combine_far(sources, table).astype(jnp.bfloat16)
    far_force = disaggregate(
        lax.all_to_all(incoming, "shard", split_axis=0, concat_axis=3, tiled=True),
        interp,
        cosine,
        sine_part,
        weights,
    )
    forcing = near_force + far_force
    return (current, forcing)


def solution(mesh):
    return jax.shard_map(
        shards,
        mesh=mesh,
        in_specs=(
            P(None, None, "space", "shard", None),
            P(None, None, "space", "shard", None),
            P("space", "shard", None),
            P(),
            P(),
            P(("space", "shard"), None),
            P(("space", "shard"), None),
            P(),
            P(),
            P(),
            P(),
            P(),
            P(),
            P(None, None, "shard"),
        ),
        out_specs=(P(None, None, "space", "shard", None), P(("space", "shard"), None, None)),
        check_vma=False,
    )
```

profile of v0, /device:TPU:0, one launch (start us, length us, event | category | flops | bytes accessed | tf_op | source)
XLA Modules:
  0.0 182.6 jit_solution(5220939384639286865)
XLA Ops:
  7.2 1.6 fusion.71
  8.8 1.6 fusion.70
  10.4 1.3 convert.41
  11.9 5.7 %convert_bitcast_fusion.7 = (bf16[1,4,16,128]{3,2,1,0:T(8,128)(2,1)S(1)}, f32[4,16,128]{2,1,0:T(8,128)}, pred[4,16,128]{2,1,0:T(8,128)(4,1)S(1)}, pred[4,16,128]...) fusion(f32[]{:T(128)} %bitcast.9, f32[]{:T(128)} %bitcast.8, ...), kind=kLoop, calls=%fused_computation.120 | loop fusion | flops 204800 | bytes 147488 | tf_op jit(solution)/shard_map/broadcast_in_dim | solution.py:132
  17.6 5.6 %convert_bitcast_fusion.6 = (bf16[1,4,16,128]{3,2,1,0:T(8,128)(2,1)S(1)}, f32[4,16,128]{2,1,0:T(8,128)}) fusion(pred[4,16,128]{2,1,0:T(8,128)(4,1)S(1)} %get-tuple-element.150, f32[]{:T(128)} %bitcast.18, pred[4,16,128]{2,1,0:T(8,128)(4,1)S(1)} %get-tuple-element.149, f32[]{:T(128)} %bitcast.17, pred[4,16,128]{2,1,0:T(8,128)(4,1)S(1)} %get-tuple-element.148, ...), kind=kLoop, calls=%fused_computation.119 | loop fusion | flops 131072 | bytes 114720 | tf_op jit(solution)/shard_map/broadcast_in_dim | solution.py:133
  23.4 1.2 fusion.67
  24.6 3.2 %collective-permute-start = (bf16[66,2,16,128]{3,2,1,0:T(8,128)(2,1)}, bf16[66,2,16,128]{3,2,1,0:T(8,128)(2,1)}, u32[]{:S(2)}, u32[]{:S(2)}) collective-permute-start(bf16[66,2,16,128]{3,2,1,0:T(8,128)(2,1)} %get-tuple-element.165), channel_id=1, source_target_pairs={{0,8},{8,16},{16,24},{1,9},{9,17},{17,25},{2,10},{10,18},{18,26},{... | collective-permute-start | bytes 1622024 | tf_op jit(solution)/shard_map/ppermute | solution.py:17
  27.8 1.3 collective-permute-start.1
  29.8 1.1 fusion.69
  30.9 2.4 %collective-permute-done.1 = bf16[66,2,16,128]{3,2,1,0:T(8,128)(2,1)} collective-permute-done((bf16[66,2,16,128]{3,2,1,0:T(8,128)(2,1)}, bf16[66,2,16,128]{3,2,1,0:T(8,128)(2,1)}, u32[]{:S(2)}, u32[]{:S(2)}) %collective-permute-start.1) | collective-permute-done | bytes 540704 | tf_op jit(solution)/shard_map/ppermute | solution.py:18
  33.3 4.5 %pad_maximum_fusion.7 = (bf16[66,8,2,128]{3,2,1,0:T(2,128)(2,1)}, bf16[66,8,2,128]{3,2,1,0:T(2,128)(2,1)}) fusion(bf16[66,2,16,128]{3,2,1,0:T(8,128)(2,1)} %collective-permute-done.1, bf16[66,2,16,128]{3,2,1,0:T(8,128)(2,1)} %collective-permute-done, bf16[1,4,16,128]{3,2,1,0:T(8,128)(2,1)} %copy-done.11, bf16[1,4,16,128]{3,2,1,0:T(8,128)(2,1)S(1)} %get-tuple-element.141, ...), kind=kLoop, calls=%fused_computation.74 | loop fusion | flops 3244032 | bytes 2703360 | tf_op jit(solution)/shard_map/slice | solution.py:15
  37.8 4.1 %collective-permute-start.2 = (bf16[66,8,2,128]{3,2,1,0:T(2,128)(2,1)}, bf16[66,8,2,128]{3,2,1,0:T(2,128)(2,1)}, u32[]{:S(2)}, u32[]{:S(2)}) collective-permute-start(bf16[66,8,2,128]{3,2,1,0:T(2,128)(2,1)} %get-tuple-element.163), channel_id=1, source_target_pairs={{0,1},{1,2},{2,3},{3,4},{4,5},{5,6},{6,7},{8,9},{9,10},{10,11},{11... | collective-permute-start | bytes 811016 | tf_op jit(solution)/shard_map/ppermute | solution.py:17
  41.9 1.5 collective-permute-start.3
  44.0 0.7 slice_bitcast_fusion.6
  44.7 0.7 collective-permute-done.2
  45.5 5.1 %collective-permute-done.3 = bf16[66,8,2,128]{3,2,1,0:T(2,128)(2,1)} collective-permute-done((bf16[66,8,2,128]{3,2,1,0:T(2,128)(2,1)}, bf16[66,8,2,128]{3,2,1,0:T(2,128)(2,1)}, u32[]{:S(2)}, u32[]{:S(2)}) %collective-permute-start.3) | collective-permute-done | bytes 270368 | tf_op jit(solution)/shard_map/ppermute | solution.py:18
  50.6 7.1 %maximum_convert_fusion = f32[66,8,20,128]{3,2,1,0:T(8,128)S(1)} fusion(bf16[66,8,2,128]{3,2,1,0:T(2,128)(2,1)} %collective-permute-done.3, bf16[66,2,16,128]{3,2,1,0:T(8,128)(2,1)} %collective-permute-done.1, bf16[1,4,16,128]{3,2,1,0:T(8,128)(2,1)} %copy-done.11, bf16[1,4,16,128]{3,2,1,0:T(8,128)(2,1)S(1)} %get-tuple-element.141, ...), kind=kLoop, calls=%fused_computation.15 | loop fusion | flops 21626880 | bytes 8110080 | tf_op jit(solution)/shard_map/convert_element_type | solution.py:137
  58.4 0.9 fusion.65
  59.3 1.1 fusion.12
  63.0 0.7 copy-done.2
  63.7 1.3 fusion.64
  65.3 12.8 %while.14 = (s32[]{:T(128)}, f32[32,2048]{1,0:T(8,128)S(1)}, bf16[32,8192]{1,0:T(8,128)(2,1)S(1)}, s32[16,128]{1,0:T(8,128)S(1)}, s32[]{:T(128)}, /*index=5*/s32[]{:T(128)}, s32[]{:T(128)}, s32[]{:T(128)}) while((s32[]{:T(128)}, f32[32,2048]{1,0:T(8,128)S(1)}, bf16[32,8192]{1,0:T(8,128)(2,1)S(1)}, s32[16,128]{1,0:T(8,128)S(1)}, ...), condition=%wide.region_1.2_spmd.clone, body=%wide.region_0.1_spmd.clone.sunk | while | flops 136446976 | bytes 606365 | solution.py:98
  65.4 1.6 fusion.80
  67.0 1.6 fusion.80
  68.6 1.6 fusion.80
  70.2 1.6 fusion.80
  71.8 1.6 fusion.80
  73.4 1.6 fusion.80
  75.0 1.6 fusion.80
  76.6 1.6 fusion.80
  79.1 1.3 fusion.16
  81.0 3.7 %copy.57 = bf16[2,16,2,2048]{1,2,0,3:T(2,128)(2,1)} copy(bf16[2,16,2,2048]{3,1,0,2:T(8,128)(2,1)S(1)} %pad_maximum_fusion.8) | data formatting | bytes 524288 | tf_op jit(solution)/shard_map/stack | solution.py:57
  84.7 4.0 %reshape.250 = bf16[8,2,8192]{2,1,0:T(2,128)(2,1)} reshape(bf16[2048,2,2,16]{3,2,1,0:T(2,128)(2,1)} %bitcast.164) | data formatting | bytes 524288
  88.8 5.2 %all-to-all-start = ((bf16[8,2,8192]{2,1,0:T(2,128)(2,1)}), bf16[8,2,8192]{2,1,0:T(2,128)(2,1)S(1)}, u32[]{:S(2)}, u32[]{:S(2)}) async-start(bf16[8,2,8192]{2,1,0:T(2,128)(2,1)} %reshape.250), calls=%async_computation | async-start | bytes 524288 | tf_op jit(solution)/shard_map/all_to_all | solution.py:190
  95.1 2.0 %gather_fusion = f32[128,2,256]{2,1,0:T(2,128)S(1)} fusion(f32[316,2,256]{2,1,0:T(2,128)} %param.31, s32[1024]{0:T(1024)S(1)} %pad_clamp_fusion.1), kind=kCustom, calls=%fused_computation.4 | custom fusion | bytes 524800 | tf_op jit(solution)/shard_map/jit(_take)/gather | solution.py:197
  97.1 5.1 %all-to-all-done = bf16[8,2,8192]{2,1,0:T(2,128)(2,1)S(1)} async-done(((bf16[8,2,8192]{2,1,0:T(2,128)(2,1)}), bf16[8,2,8192]{2,1,0:T(2,128)(2,1)S(1)}, u32[]{:S(2)}, u32[]{:S(2)}) %all-to-all-start) | async-done | bytes 262176 | tf_op jit(solution)/shard_map/all_to_all | solution.py:190
  102.2 2.4 %reshape.251 = bf16[2048,2,2,16]{3,2,1,0:T(2,128)(2,1)} reshape(bf16[8,2,8192]{2,1,0:T(2,128)(2,1)S(1)} %all-to-all-done) | data formatting | bytes 524288
  104.5 5.6 %copy.65 = bf16[2,16,2,8,256]{4,1,2,0,3:T(8,128)(2,1)} copy(bf16[2,16,2,8,256]{1,2,0,4,3:T(2,128)(2,1)} %bitcast.165) | data formatting | bytes 524288 | tf_op jit(solution)/shard_map/all_to_all | solution.py:190
  111.3 1.9 %collective-permute-start.4 = (bf16[16,16,256]{2,1,0:T(8,128)(2,1)S(1)}, bf16[16,16,256]{2,1,0:T(8,128)(2,1)S(1)}, u32[]{:S(2)}, u32[]{:S(2)}) collective-permute-start(bf16[16,16,256]{2,1,0:T(8,128)(2,1)S(1)} %reshape.177), channel_id=1, source_target_pairs={{0,1},{1,2},{2,3},{3,4},{4,5},{5,6},{6,7},{8,9},{9,10},{10,11},{11... | collective-permute-start | bytes 393224 | tf_op jit(solution)/shard_map/ppermute | solution.py:17
  113.3 0.7 copy.54
  114.7 1.2 pad_clamp_fusion.2
  115.9 1.3 collective-permute-start.5
  117.3 5.5 %collective-permute-done.5 = bf16[16,16,256]{2,1,0:T(8,128)(2,1)S(1)} collective-permute-done((bf16[16,16,256]{2,1,0:T(8,128)(2,1)S(1)}, bf16[16,16,256]{2,1,0:T(8,128)(2,1)S(1)}, u32[]{:S(2)}, u32[]{:S(2)}) %collective-permute-start.5) | collective-permute-done | bytes 131104 | tf_op jit(solution)/shard_map/ppermute | solution.py:18
  122.8 1.3 gather_fusion.5
  124.1 1.3 gather_fusion.4
  125.5 1.2 gather_fusion.3
  126.7 1.2 gather_fusion.2
  127.9 1.1 fusion.38
  129.0 1.8 all-gather.2.cloned.1.call-done
  130.8 3.2 %gather_fusion.1 = bf16[128,16,2,256]{3,1,2,0:T(8,128)(2,1)} fusion(bf16[64,16,2,256]{3,1,2,0:T(8,128)(2,1)} %all-gather.2.cloned.1.call-done, s32[1024]{0:T(1024)S(1)} %pad_clamp_fusion), kind=kCustom, calls=%fused_computation.5 | custom fusion | bytes 4194816 | tf_op jit(solution)/shard_map/jit(_take)/gather | solution.py:199
  134.1 2.0 %select_convert_fusion = f32[16,8,16,2,256]{4,2,3,1,0:T(8,128)S(1)} fusion(bf16[16,8,16,2,256]{4,2,3,1,0:T(8,128)(2,1)} %bitcast.166, pred[16,8]{1,0:T(8,128)(4,1)S(1)} %copy.54), kind=kLoop, calls=%fused_computation.37 | loop fusion | flops 2097152 | bytes 6291584 | tf_op jit(solution)/shard_map/convert_element_type | solution.py:199
  136.1 0.8 subtract_reduce_fusion
  136.8 0.7 pad_maximum_fusion.9
  137.6 5.5 %all-to-all-start.1 = ((bf16[16,16,2,256]{3,1,2,0:T(8,128)(2,1)}), bf16[16,16,2,256]{3,1,2,0:T(8,128)(2,1)S(1)}, u32[]{:S(2)}, u32[]{:S(2)}) async-start(bf16[16,16,2,256]{3,1,2,0:T(8,128)(2,1)} %pad_maximum_fusion.9), calls=%async_computation.1 | async-start | bytes 524288 | tf_op jit(solution)/shard_map/all_to_all | solution.py:202
  143.1 1.8 %fusion.36 = f32[16,16,256]{2,1,0:T(8,128)} fusion(bf16[16,16,256]{2,1,0:T(8,128)(2,1)} %gather_fusion.4, bf16[4,256,256]{2,1,0:T(8,128)(2,1)S(1)} %copy-done.6, pred[16]{0:T(512)(128)(4,1)S(1)} %copy-done.25), kind=kOutput, calls=%fused_computation.86 | convolution fusion | flops 33619968 | bytes 524800 | tf_op jit(solution)/shard_map/dot_general | solution.py:176
  144.9 0.9 fusion.34
  145.9 6.5 %all-to-all-done.1 = bf16[16,16,2,256]{3,1,2,0:T(8,128)(2,1)S(1)} async-done(((bf16[16,16,2,256]{3,1,2,0:T(8,128)(2,1)}), bf16[16,16,2,256]{3,1,2,0:T(8,128)(2,1)S(1)}, u32[]{:S(2)}, u32[]{:S(2)}) %all-to-all-start.1) | async-done | bytes 262176 | tf_op jit(solution)/shard_map/all_to_all | solution.py:202
  152.9 4.4 %add_convert_fusion = (bf16[2,8,16,1,2048]{4,3,2,1,0:T(2,128)(2,1)S(1)}, bf16[2,8,16,1,2048]{4,3,2,1,0:T(2,128)(2,1)S(1)}) fusion(f32[2,16,2048]{2,1,0:T(8,128)S(1)} %get-tuple-element.170, f32[8,2048]{1,0:T(8,128)S(1)} %get-tuple-element.178, f32[2,16,2048]{2,1,0:T(8,128)S(1)} %get-tuple-element.169, f32[8,2048]{1,0:T(8,128)S(1)} %get-tuple-element.177), kind=kLoop, calls=%fused_computation.34 | loop fusion | flops 4194304 | bytes 2752512 | tf_op jit(solution)/shard_map/convert.3
  157.3 5.2 %pad_maximum_fusion = bf16[2,8,16,2,2048]{4,3,2,1,0:T(2,128)(2,1)} fusion(bf16[2,8,16,1,2048]{4,3,2,1,0:T(2,128)(2,1)S(1)} %get-tuple-element.168, bf16[2,8,16,1,2048]{4,3,2,1,0:T(2,128)(2,1)S(1)} %get-tuple-element.167), kind=kLoop, calls=%fused_computation.30 | loop fusion | flops 4194304 | bytes 4194304 | tf_op jit(solution)/shard_map/stack | solution.py:76
  162.5 4.1 %convert_element_type.61 = bf16[512,2048]{1,0:T(8,128)(2,1)} reshape(bf16[2,8,16,2,2048]{4,3,2,1,0:T(2,128)(2,1)} %pad_maximum_fusion) | data formatting | bytes 4194304 | tf_op jit(solution)/shard_map/convert_element_type | solution.py:76
  166.6 3.7 %convolution_convert_fusion = bf16[512,512]{1,0:T(8,128)(2,1)} fusion(bf16[512,2048]{1,0:T(8,128)(2,1)} %convert_element_type.61, bf16[512,2048]{1,0:T(8,128)(2,1)S(1)} %copy-done), kind=kOutput, calls=%fused_computation.40 | convolution fusion | flops 1074003968 | bytes 4718592 | tf_op jit(solution)/shard_map/dot_general | solution.py:77
  170.3 2.1 %dot_general.43 = bf16[16,16,1024]{2,1,0:T(8,128)(2,1)} reshape(bf16[512,512]{1,0:T(8,128)(2,1)} %convolution_convert_fusion) | data formatting | bytes 1048576 | tf_op jit(solution)/shard_map/dot_general | solution.py:81
  172.4 1.4 fusion.29
  173.9 1.9 %fusion.22 = f32[16,16,256]{2,1,0:T(8,128)} fusion(f32[16,16,256]{2,1,0:T(8,128)S(1)} %fusion.29, f32[16,16,256]{2,1,0:T(8,128)S(1)} %copy-done.4, f32[16,16,256]{2,1,0:T(8,128)S(1)} %copy-done.3, f32[16,16,256]{2,1,0:T(8,128)S(1)} %fusion.38, bf16[16,16,256]{2,1,0:T(8,128)(2,1)S(1)} %copy-done.7, bf16[4,256,256]{2,1,0:T(8,128)(2,1)} %param.25, ...), kind=kOutput, calls=%fused_computation.49 | convolution fusion | flops 33882112 | bytes 1572880 | tf_op jit(solution)/shard_map/dot_general | solution.py:176
  (114 shorter events, 10.1 us)
Async XLA Ops:
  7.2 71.9 %copy-start = (bf16[512,2048]{1,0:T(8,128)(2,1)S(1)}, bf16[512,2048]{1,0:T(8,128)(2,1)}, u32[]{:S(2)}) copy-start(bf16[512,2048]{1,0:T(8,128)(2,1)} %param.27) | copy-start | bytes 6291460
  7.2 4.6 %copy-start.1 = (f32[2,16,4,16,128]{4,3,2,1,0:T(8,128)S(1)}, f32[2,16,4,16,128]{4,3,2,1,0:T(8,128)}, u32[]{:S(2)}) copy-start(f32[2,16,4,16,128]{4,3,2,1,0:T(8,128)} %param.19) | copy-start | bytes 3145732
  7.2 4.7 %copy-start.19 = (s32[4,16,128]{2,1,0:T(8,128)S(1)}, s32[4,16,128]{2,1,0:T(8,128)}, u32[]{:S(2)}) copy-start(s32[4,16,128]{2,1,0:T(8,128)} %param.20) | copy-start | bytes 98308
  23.2 1.4 copy-start.11
  23.2 5.9 %copy-start.5 = (bf16[2,128,512]{2,1,0:T(8,128)(2,1)S(1)}, bf16[2,128,512]{2,1,0:T(8,128)(2,1)}, u32[]{:S(2)}) copy-start(bf16[2,128,512]{2,1,0:T(8,128)(2,1)} %param.26) | copy-start | bytes 786436
  24.6 6.3 %collective-permute-start = (bf16[66,2,16,128]{3,2,1,0:T(8,128)(2,1)}, bf16[66,2,16,128]{3,2,1,0:T(8,128)(2,1)}, u32[]{:S(2)}, u32[]{:S(2)}) collective-permute-start(bf16[66,2,16,128]{3,2,1,0:T(8,128)(2,1)} %get-tuple-element.165), channel_id=1, source_target_pairs={{0,8},{8,16},{16,24},{1,9},{9,17},{17,25},{2,10},{10,18},{18,26},{... | collective-permute-start | bytes 1622024 | tf_op jit(solution)/shard_map/ppermute | solution.py:17
  27.8 5.5 %collective-permute-start.1 = (bf16[66,2,16,128]{3,2,1,0:T(8,128)(2,1)}, bf16[66,2,16,128]{3,2,1,0:T(8,128)(2,1)}, u32[]{:S(2)}, u32[]{:S(2)}) collective-permute-start(bf16[66,2,16,128]{3,2,1,0:T(8,128)(2,1)} %get-tuple-element.166), channel_id=1, source_target_pairs={{8,0},{16,8},{24,16},{9,1},{17,9},{25,17},{10,2},{18,10},{26,18},{... | collective-permute-start | bytes 1622024 | tf_op jit(solution)/shard_map/ppermute | solution.py:18
  37.8 7.7 %collective-permute-start.2 = (bf16[66,8,2,128]{3,2,1,0:T(2,128)(2,1)}, bf16[66,8,2,128]{3,2,1,0:T(2,128)(2,1)}, u32[]{:S(2)}, u32[]{:S(2)}) collective-permute-start(bf16[66,8,2,128]{3,2,1,0:T(2,128)(2,1)} %get-tuple-element.163), channel_id=1, source_target_pairs={{0,1},{1,2},{2,3},{3,4},{4,5},{5,6},{6,7},{8,9},{9,10},{10,11},{11... | collective-permute-start | bytes 811016 | tf_op jit(solution)/shard_map/ppermute | solution.py:17
  41.9 8.7 %collective-permute-start.3 = (bf16[66,8,2,128]{3,2,1,0:T(2,128)(2,1)}, bf16[66,8,2,128]{3,2,1,0:T(2,128)(2,1)}, u32[]{:S(2)}, u32[]{:S(2)}) collective-permute-start(bf16[66,8,2,128]{3,2,1,0:T(2,128)(2,1)} %get-tuple-element.164), channel_id=1, source_target_pairs={{1,0},{2,1},{3,2},{4,3},{5,4},{6,5},{7,6},{9,8},{10,9},{11,10},{12... | collective-permute-start | bytes 811016 | tf_op jit(solution)/shard_map/ppermute | solution.py:18
  44.7 12.9 %copy-start.20 = (pred[6,18]{1,0:T(8,128)(4,1)S(1)}, pred[6,18]{1,0:T(8,128)(4,1)}, u32[]{:S(2)}) copy-start(pred[6,18]{1,0:T(8,128)(4,1)} %broadcast_and_fusion) | copy-start | bytes 328
  61.9 0.8 copy-start.10
  61.9 0.8 copy-start.13
  62.5 1.2 copy-start.2
  63.7 1.6 copy-start.12
  63.7 1.6 copy-start.27
  65.3 13.1 %copy-start.14 = (bf16[128,512]{1,0:T(8,128)(2,1)S(1)}, bf16[128,512]{1,0:T(8,128)(2,1)}, u32[]{:S(2)}) copy-start(bf16[128,512]{1,0:T(8,128)(2,1)} %fusion.63) | copy-start | bytes 393220
  65.3 13.1 %copy-start.16 = (bf16[128,512]{1,0:T(8,128)(2,1)S(1)}, bf16[128,512]{1,0:T(8,128)(2,1)}, u32[]{:S(2)}) copy-start(bf16[128,512]{1,0:T(8,128)(2,1)} %get-tuple-element.173) | copy-start | bytes 393220
  65.3 13.1 %copy-start.18 = (bf16[128,512]{1,0:T(8,128)(2,1)S(1)}, bf16[128,512]{1,0:T(8,128)(2,1)}, u32[]{:S(2)}) copy-start(bf16[128,512]{1,0:T(8,128)(2,1)} %get-tuple-element.174) | copy-start | bytes 393220
  81.0 13.0 %copy-start.21 = (s32[64,8]{0,1:T(8,128)S(1)}, s32[64,8]{0,1:T(8,128)}, u32[]{:S(2)}) copy-start(s32[64,8]{0,1:T(8,128)} %param.29) | copy-start | bytes 6148
  81.0 13.0 %copy-start.22 = (s32[64,8]{0,1:T(8,128)S(1)}, s32[64,8]{0,1:T(8,128)}, u32[]{:S(2)}) copy-start(s32[64,8]{0,1:T(8,128)} %param.30) | copy-start | bytes 6148
  84.7 12.4 %copy-start.26 = (s32[16,4]{0,1:T(4,128)S(1)}, s32[16,4]{0,1:T(4,128)}, u32[]{:S(2)}) copy-start(s32[16,4]{0,1:T(4,128)} %param.24) | copy-start | bytes 772
  88.8 13.4 %all-to-all-start = ((bf16[8,2,8192]{2,1,0:T(2,128)(2,1)}), bf16[8,2,8192]{2,1,0:T(2,128)(2,1)S(1)}, u32[]{:S(2)}, u32[]{:S(2)}) async-start(bf16[8,2,8192]{2,1,0:T(2,128)(2,1)} %reshape.250), calls=%async_computation | async-start | bytes 524288 | tf_op jit(solution)/shard_map/all_to_all | solution.py:190
  93.9 36.9 %all-gather.2.cloned.1.call-start = ((), (), s32[]{:S(2)}) async-start(), calls=%async_computation.2 | async-start | bytes 1310720 | tf_op jit(solution)/shard_map/all_gather | solution.py:198
  110.2 17.7 %copy-start.6 = (bf16[4,256,256]{2,1,0:T(8,128)(2,1)S(1)}, bf16[4,256,256]{2,1,0:T(8,128)(2,1)}, u32[]{:S(2)}) copy-start(bf16[4,256,256]{2,1,0:T(8,128)(2,1)} %param.25) | copy-start | bytes 1572868
  111.3 5.9 %collective-permute-start.4 = (bf16[16,16,256]{2,1,0:T(8,128)(2,1)S(1)}, bf16[16,16,256]{2,1,0:T(8,128)(2,1)S(1)}, u32[]{:S(2)}, u32[]{:S(2)}) collective-permute-start(bf16[16,16,256]{2,1,0:T(8,128)(2,1)S(1)} %reshape.177), channel_id=1, source_target_pairs={{0,1},{1,2},{2,3},{3,4},{4,5},{5,6},{6,7},{8,9},{9,10},{10,11},{11... | collective-permute-start | bytes 393224 | tf_op jit(solution)/shard_map/ppermute | solution.py:17
  115.9 6.8 %collective-permute-start.5 = (bf16[16,16,256]{2,1,0:T(8,128)(2,1)S(1)}, bf16[16,16,256]{2,1,0:T(8,128)(2,1)S(1)}, u32[]{:S(2)}, u32[]{:S(2)}) collective-permute-start(bf16[16,16,256]{2,1,0:T(8,128)(2,1)S(1)} %reshape.177), channel_id=1, source_target_pairs={{1,0},{2,1},{3,2},{4,3},{5,4},{6,5},{7,6},{9,8},{10,9},{11,10},{12... | collective-permute-start | bytes 393224 | tf_op jit(solution)/shard_map/ppermute | solution.py:18
  134.1 2.0 %copy-start.8 = (f32[16,8,1,256]{3,1,2,0:T(8,128)S(1)}, f32[16,8,1,256]{3,1,2,0:T(8,128)}, u32[]{:S(2)}) copy-start(f32[16,8,1,256]{3,1,2,0:T(8,128)} %copy.82) | copy-start | bytes 393220
  136.0 7.1 %copy-start.25 = (pred[16]{0:T(512)(128)(4,1)S(1)}, pred[16]{0:T(512)(128)(4,1)}, u32[]{:S(2)}) copy-start(pred[16]{0:T(512)(128)(4,1)} %get-tuple-element.181) | copy-start | bytes 52
  136.0 8.9 %copy-start.9 = (bf16[16,16,256]{2,1,0:T(8,128)(2,1)S(1)}, bf16[16,16,256]{2,1,0:T(8,128)(2,1)}, u32[]{:S(2)}) copy-start(bf16[16,16,256]{2,1,0:T(8,128)(2,1)} %gather_fusion.5) | copy-start | bytes 393220
  136.1 8.9 %copy-start.24 = (pred[16]{0:T(512)(128)(4,1)S(1)}, pred[16]{0:T(512)(128)(4,1)}, u32[]{:S(2)}) copy-start(pred[16]{0:T(512)(128)(4,1)} %get-tuple-element.179) | copy-start | bytes 52
  137.6 14.8 %all-to-all-start.1 = ((bf16[16,16,2,256]{3,1,2,0:T(8,128)(2,1)}), bf16[16,16,2,256]{3,1,2,0:T(8,128)(2,1)S(1)}, u32[]{:S(2)}, u32[]{:S(2)}) async-start(bf16[16,16,2,256]{3,1,2,0:T(8,128)(2,1)} %pad_maximum_fusion.9), calls=%async_computation.1 | async-start | bytes 524288 | tf_op jit(solution)/shard_map/all_to_all | solution.py:202
  166.6 5.8 %copy-start.15 = (bf16[128,512]{1,0:T(8,128)(2,1)S(1)}, bf16[128,512]{1,0:T(8,128)(2,1)}, u32[]{:S(2)}) copy-start(bf16[128,512]{1,0:T(8,128)(2,1)} %fusion.63) | copy-start | bytes 393220
  166.6 5.8 %copy-start.17 = (bf16[128,512]{1,0:T(8,128)(2,1)S(1)}, bf16[128,512]{1,0:T(8,128)(2,1)}, u32[]{:S(2)}) copy-start(bf16[128,512]{1,0:T(8,128)(2,1)} %get-tuple-element.173) | copy-start | bytes 393220
  170.3 3.5 %copy-start.3 = (f32[16,16,256]{2,1,0:T(8,128)S(1)}, f32[16,16,256]{2,1,0:T(8,128)}, u32[]{:S(2)}) copy-start(f32[16,16,256]{2,1,0:T(8,128)} %fusion.36) | copy-start | bytes 786436
  170.3 3.5 %copy-start.4 = (f32[16,16,256]{2,1,0:T(8,128)S(1)}, f32[16,16,256]{2,1,0:T(8,128)}, u32[]{:S(2)}) copy-start(f32[16,16,256]{2,1,0:T(8,128)} %fusion.34) | copy-start | bytes 786436
  170.3 3.5 %copy-start.7 = (bf16[16,16,256]{2,1,0:T(8,128)(2,1)S(1)}, bf16[16,16,256]{2,1,0:T(8,128)(2,1)}, u32[]{:S(2)}) copy-start(bf16[16,16,256]{2,1,0:T(8,128)(2,1)} %gather_fusion.2) | copy-start | bytes 393220
  170.3 3.6 %copy-start.23 = (pred[16]{0:T(512)(128)(4,1)S(1)}, pred[16]{0:T(512)(128)(4,1)}, u32[]{:S(2)}) copy-start(pred[16]{0:T(512)(128)(4,1)} %get-tuple-element.127) | copy-start | bytes 52
Sparse Core Ops, SparseCore 0:
  110.3 20.4 all-gather.1
where the time goes:
time: 184 us; the launch traced here: 183 us
  other arithmetic  46.8 us (25%)
  local copies, waits for them, and re-layouts  44.7 us (24%)
  waiting for transfers between devices  27.1 us (15%)
  matrix products  25 us (14%)
  starting transfers between devices  23.9 us (13%)
  between operations  14.7 us (8%)
    ppermute x3, waiting for transfers between devices, padded_2(): after = lax.ppermute(leading, axis, down)  13 us
    dot_general x8, matrix products, add_block(): return total + jnp.dot(piece, selector, preferred_element_type=jnp.float32)  12.5 us
    ppermute x3, starting transfers between devices, padded_2(): before = lax.ppermute(last, axis, up)  9.22 us
    unnamed x63, local copies, waits for them, and re-layouts  8.24 us
    convert_element_type x1, other arithmetic, shards(): padded_2(stacked.astype(jnp.bfloat16), (('space', 1), ('shard', 2)), 2)  7.05 us
    all_to_all x1, waiting for transfers between devices, shards(): lax.all_to_all(incoming, 'shard', split_axis=0, concat_axis=3, tiled=True)  6.52 us
    another operation x3, other arithmetic  5.8 us
    dot_general x4, matrix products, shards(): jnp.dot(picked, near_blocks[slot_index], preferred_element_type=jnp.float32)  5.76 us
  transfers between devices with their start and end apart: 9, of which 7 were waited for; matrix products, arithmetic and copies ran while one was open for 10% of the time, Pallas kernels for 0%

commit v1 on v0

--- a/solution.py
+++ b/solution.py
@@ -187,7 +187,28 @@
     cosine = jnp.cos(phase_angle)
     sine_part = jnp.sin(phase_angle)
     parent_patterns = aggregate(leaf, interp, cosine, sine_part)
-    directed = lax.all_to_all(parent_patterns, "shard", split_axis=3, concat_axis=0, tiled=True)
+    top = lax.axis_size("shard")
+    outcome_arr = lax.axis_index("shard")
+    seen_now, wide_out = (top, outcome_arr)
+    value_now = parent_patterns.shape[3] // seen_now
+    item_now = list(parent_patterns.shape)
+    item_now[3] = value_now
+    z2 = item_now[0]
+    item_now[0] = z2 * seen_now
+    directed = jnp.zeros(item_now, parent_patterns.dtype)
+    no = 0
+    while no < seen_now:
+        next_value = lax.dynamic_slice_in_dim(
+            parent_patterns, (wide_out ^ no) * value_now, value_now, axis=3
+        )
+        if no:
+            next_value = lax.ppermute(
+                next_value, "shard", [(nth, nth ^ no) for nth in range(seen_now)]
+            )
+        directed = lax.dynamic_update_slice_in_dim(
+            directed, next_value, (wide_out ^ no) * z2, axis=0
+        )
+        no += 1
     group_parents = directed.shape[0]
     group_index = lax.axis_index("space")
     target_ids = lax.dynamic_slice_in_dim(

time: 184 us -> 187 us (1.016)
  local copies, waits for them, and re-layouts: 44.7 us -> 30.5 us
  matrix products: 25 us -> 38.1 us
  starting transfers between devices: 23.9 us -> 33 us
  waiting for transfers between devices: 27.1 us -> 22.8 us
    ppermute x0 -> x7, starting transfers between devices: none -> 12.9 us  [shards(): lax.ppermute(next_value, 'shard', [(nth, nth ^ no) for nth in range(seen_...]
    dot_general x8, matrix products: 12.5 us -> 24.7 us  [add_block(): return total + jnp.dot(piece, selector, preferred_element_type=jnp.float32)]
    ppermute x3, waiting for transfers between devices: 13 us -> 6.3 us  [padded_2(): after = lax.ppermute(leading, axis, down)]
    unnamed x63, local copies, waits for them, and re-layouts: 8.24 us -> 2.49 us
    all_to_all x1 -> x0, local copies, waits for them, and re-layouts: 5.63 us -> none  [shards(): lax.all_to_all(parent_patterns, 'shard', split_axis=3, concat_axis=0, til...]
    all_to_all x1 -> x0, starting transfers between devices: 5.16 us -> none  [shards(): lax.all_to_all(parent_patterns, 'shard', split_axis=3, concat_axis=0, til...]
    all_to_all x1 -> x0, waiting for transfers between devices: 5.06 us -> none  [shards(): lax.all_to_all(parent_patterns, 'shard', split_axis=3, concat_axis=0, til...]
    ppermute x0 -> x7, waiting for transfers between devices: none -> 4.54 us  [shards(): lax.ppermute(next_value, 'shard', [(nth, nth ^ no) for nth in range(seen_...]
  transfers between devices with their start and end apart: 9 -> 15, of which waited for: 7 -> 9; matrix products, arithmetic and copies ran while one was open for 10% -> 10% of each run, Pallas kernels for 0% -> 0%
where the time goes in v1:
time: 187 us; the launch traced here: 186 us
  other arithmetic  47 us (25%)
  matrix products  38.1 us (20%)
  starting transfers between devices  33 us (18%)
  local copies, waits for them, and re-layouts  30.5 us (16%)
  waiting for transfers between devices  22.8 us (12%)
  between operations  14.8 us (8%)
    dot_general x8, matrix products, add_block(): return total + jnp.dot(piece, selector, preferred_element_type=jnp.float32)  24.7 us
    ppermute x7, starting transfers between devices, shards(): lax.ppermute(next_value, 'shard', [(nth, nth ^ no) for nth in range(seen_...  12.9 us
    ppermute x3, starting transfers between devices, padded_2(): before = lax.ppermute(last, axis, up)  10.6 us
    convert_element_type x1, other arithmetic, shards(): padded_2(stacked.astype(jnp.bfloat16), (('space', 1), ('shard', 2)), 2)  7.05 us
    dot_general x4, matrix products, shards(): jnp.dot(picked, near_blocks[slot_index], preferred_element_type=jnp.float32)  6.67 us
    ppermute x3, waiting for transfers between devices, padded_2(): after = lax.ppermute(leading, axis, down)  6.3 us
    another operation x3, other arithmetic  5.8 us
    broadcast_in_dim x1, other arithmetic, shards(): diagonal_coef[None]  5.68 us
  transfers between devices with their start and end apart: 15, of which 9 were waited for; matrix products, arithmetic and copies ran while one was open for 10% of the time, Pallas kernels for 0%

profile of v1, /device:TPU:0, one launch (start us, length us, event | category | flops | bytes accessed | tf_op | source)
XLA Modules:
  0.0 186.2 jit_solution(2825481755675530046)
XLA Ops:
  7.2 1.6 fusion.79
  8.9 1.6 fusion.78
  10.5 1.3 convert.41
  11.9 5.7 %convert_bitcast_fusion.7 = (bf16[1,4,16,128]{3,2,1,0:T(8,128)(2,1)S(1)}, f32[4,16,128]{2,1,0:T(8,128)}, pred[4,16,128]{2,1,0:T(8,128)(4,1)S(1)}, pred[4,16,128]...) fusion(f32[]{:T(128)} %bitcast.9, f32[]{:T(128)} %bitcast.8, ...), kind=kLoop, calls=%fused_computation.151 | loop fusion | flops 204800 | bytes 147488 | tf_op jit(solution)/shard_map/broadcast_in_dim | solution.py:132
  17.6 5.6 %convert_bitcast_fusion.6 = (bf16[1,4,16,128]{3,2,1,0:T(8,128)(2,1)S(1)}, f32[4,16,128]{2,1,0:T(8,128)}) fusion(pred[4,16,128]{2,1,0:T(8,128)(4,1)S(1)} %get-tuple-element.150, f32[]{:T(128)} %bitcast.18, pred[4,16,128]{2,1,0:T(8,128)(4,1)S(1)} %get-tuple-element.149, f32[]{:T(128)} %bitcast.17, pred[4,16,128]{2,1,0:T(8,128)(4,1)S(1)} %get-tuple-element.148, ...), kind=kLoop, calls=%fused_computation.150 | loop fusion | flops 131072 | bytes 114720 | tf_op jit(solution)/shard_map/broadcast_in_dim | solution.py:133
  23.5 1.2 fusion.75
  24.6 3.2 %collective-permute-start = (bf16[66,2,16,128]{3,2,1,0:T(8,128)(2,1)}, bf16[66,2,16,128]{3,2,1,0:T(8,128)(2,1)}, u32[]{:S(2)}, u32[]{:S(2)}) collective-permute-start(bf16[66,2,16,128]{3,2,1,0:T(8,128)(2,1)} %get-tuple-element.165), channel_id=1, source_target_pairs={{0,8},{8,16},{16,24},{1,9},{9,17},{17,25},{2,10},{10,18},{18,26},{... | collective-permute-start | bytes 1622024 | tf_op jit(solution)/shard_map/ppermute | solution.py:17
  27.9 1.3 collective-permute-start.1
  31.8 1.1 fusion.77
  33.3 4.5 %pad_maximum_fusion.7 = (bf16[66,8,2,128]{3,2,1,0:T(2,128)(2,1)}, bf16[66,8,2,128]{3,2,1,0:T(2,128)(2,1)}) fusion(bf16[66,2,16,128]{3,2,1,0:T(8,128)(2,1)} %collective-permute-done.1, bf16[66,2,16,128]{3,2,1,0:T(8,128)(2,1)} %collective-permute-done, bf16[1,4,16,128]{3,2,1,0:T(8,128)(2,1)} %copy-done.12, bf16[1,4,16,128]{3,2,1,0:T(8,128)(2,1)S(1)} %get-tuple-element.141, ...), kind=kLoop, calls=%fused_computation.90 | loop fusion | flops 3244032 | bytes 2703360 | tf_op jit(solution)/shard_map/slice | solution.py:15
  37.8 4.6 %collective-permute-start.2 = (bf16[66,8,2,128]{3,2,1,0:T(2,128)(2,1)}, bf16[66,8,2,128]{3,2,1,0:T(2,128)(2,1)}, u32[]{:S(2)}, u32[]{:S(2)}) collective-permute-start(bf16[66,8,2,128]{3,2,1,0:T(2,128)(2,1)} %get-tuple-element.163), channel_id=1, source_target_pairs={{0,1},{1,2},{2,3},{3,4},{4,5},{5,6},{6,7},{8,9},{9,10},{10,11},{11... | collective-permute-start | bytes 811016 | tf_op jit(solution)/shard_map/ppermute | solution.py:17
  42.4 1.5 collective-permute-start.3
  45.8 2.1 %gather_fusion = f32[128,2,256]{2,1,0:T(2,128)S(1)} fusion(f32[316,2,256]{2,1,0:T(2,128)} %param.31, s32[1024]{0:T(1024)} %pad_clamp_fusion.1), kind=kCustom, calls=%fused_computation.4 | custom fusion | bytes 524800 | tf_op jit(solution)/shard_map/jit(_take)/gather | solution.py:218
  47.9 1.7 slice_bitcast_fusion.6
  49.6 1.4 collective-permute-done.3
  51.0 7.1 %maximum_convert_fusion = f32[66,8,20,128]{3,2,1,0:T(8,128)S(1)} fusion(bf16[66,8,2,128]{3,2,1,0:T(2,128)(2,1)} %collective-permute-done.3, bf16[66,2,16,128]{3,2,1,0:T(8,128)(2,1)} %collective-permute-done.1, bf16[1,4,16,128]{3,2,1,0:T(8,128)(2,1)} %copy-done.12, bf16[1,4,16,128]{3,2,1,0:T(8,128)(2,1)S(1)} %get-tuple-element.141, ...), kind=kLoop, calls=%fused_computation.15 | loop fusion | flops 21626880 | bytes 8110080 | tf_op jit(solution)/shard_map/convert_element_type | solution.py:137
  58.9 0.9 fusion.73
  59.8 1.1 fusion.12
  63.4 0.7 copy-done.2
  64.2 1.3 fusion.72
  65.8 24.8 %while.14 = (s32[]{:T(128)}, f32[32,2048]{1,0:T(8,128)}, bf16[32,8192]{1,0:T(8,128)(2,1)S(1)}, s32[16,128]{1,0:T(8,128)S(1)}, s32[]{:T(128)}, /*index=5*/s32[]{:T(128)}, s32[]{:T(128)}, s32[]{:T(128)}) while((s32[]{:T(128)}, f32[32,2048]{1,0:T(8,128)}, bf16[32,8192]{1,0:T(8,128)(2,1)S(1)}, s32[16,128]{1,0:T(8,128)S(1)}, s32[]{:T(128)}, ...), condition=%wide.region_1.2_spmd.clone, body=%wide.region_0.1_spmd.clone.sunk | while | flops 136446976 | bytes 606365 | solution.py:98
  65.8 2.3 %fusion.88 = f32[32,2048]{1,0:T(8,128)} fusion(s32[2048]{0:T(1024)S(1)} %bitcast.177, s32[1024]{0:T(1024)S(1)} %iota_add_fusion.2, f32[32,2048]{1,0:T(8,128)} %get-tuple-element.249, pred[]{:T(512)S(6)} %compare.7, bf16[32,8192]{1,0:T(8,128)(2,1)S(1)} %get-tuple-element.258, s32[]{:T(128)S(6)} %select_n.260), kind=kOutput, calls=%fused_computation.11.clone.1 | convolution fusion | flops 136445952 | bytes 602117 | tf_op jit(solution)/shard_map/while/body/eval_jaxpr/dot_general | solution.py:95
  68.1 3.2 %fusion.88 = f32[32,2048]{1,0:T(8,128)} fusion(s32[2048]{0:T(1024)S(1)} %bitcast.177, s32[1024]{0:T(1024)S(1)} %iota_add_fusion.2, f32[32,2048]{1,0:T(8,128)} %get-tuple-element.249, pred[]{:T(512)S(6)} %compare.7, bf16[32,8192]{1,0:T(8,128)(2,1)S(1)} %get-tuple-element.258, s32[]{:T(128)S(6)} %select_n.260), kind=kOutput, calls=%fused_computation.11.clone.1 | convolution fusion | flops 136445952 | bytes 602117 | tf_op jit(solution)/shard_map/while/body/eval_jaxpr/dot_general | solution.py:95
  71.3 3.2 %fusion.88 = f32[32,2048]{1,0:T(8,128)} fusion(s32[2048]{0:T(1024)S(1)} %bitcast.177, s32[1024]{0:T(1024)S(1)} %iota_add_fusion.2, f32[32,2048]{1,0:T(8,128)} %get-tuple-element.249, pred[]{:T(512)S(6)} %compare.7, bf16[32,8192]{1,0:T(8,128)(2,1)S(1)} %get-tuple-element.258, s32[]{:T(128)S(6)} %select_n.260), kind=kOutput, calls=%fused_computation.11.clone.1 | convolution fusion | flops 136445952 | bytes 602117 | tf_op jit(solution)/shard_map/while/body/eval_jaxpr/dot_general | solution.py:95
  74.5 3.2 %fusion.88 = f32[32,2048]{1,0:T(8,128)} fusion(s32[2048]{0:T(1024)S(1)} %bitcast.177, s32[1024]{0:T(1024)S(1)} %iota_add_fusion.2, f32[32,2048]{1,0:T(8,128)} %get-tuple-element.249, pred[]{:T(512)S(6)} %compare.7, bf16[32,8192]{1,0:T(8,128)(2,1)S(1)} %get-tuple-element.258, s32[]{:T(128)S(6)} %select_n.260), kind=kOutput, calls=%fused_computation.11.clone.1 | convolution fusion | flops 136445952 | bytes 602117 | tf_op jit(solution)/shard_map/while/body/eval_jaxpr/dot_general | solution.py:95
  77.7 3.2 %fusion.88 = f32[32,2048]{1,0:T(8,128)} fusion(s32[2048]{0:T(1024)S(1)} %bitcast.177, s32[1024]{0:T(1024)S(1)} %iota_add_fusion.2, f32[32,2048]{1,0:T(8,128)} %get-tuple-element.249, pred[]{:T(512)S(6)} %compare.7, bf16[32,8192]{1,0:T(8,128)(2,1)S(1)} %get-tuple-element.258, s32[]{:T(128)S(6)} %select_n.260), kind=kOutput, calls=%fused_computation.11.clone.1 | convolution fusion | flops 136445952 | bytes 602117 | tf_op jit(solution)/shard_map/while/body/eval_jaxpr/dot_general | solution.py:95
  80.9 3.2 %fusion.88 = f32[32,2048]{1,0:T(8,128)} fusion(s32[2048]{0:T(1024)S(1)} %bitcast.177, s32[1024]{0:T(1024)S(1)} %iota_add_fusion.2, f32[32,2048]{1,0:T(8,128)} %get-tuple-element.249, pred[]{:T(512)S(6)} %compare.7, bf16[32,8192]{1,0:T(8,128)(2,1)S(1)} %get-tuple-element.258, s32[]{:T(128)S(6)} %select_n.260), kind=kOutput, calls=%fused_computation.11.clone.1 | convolution fusion | flops 136445952 | bytes 602117 | tf_op jit(solution)/shard_map/while/body/eval_jaxpr/dot_general | solution.py:95
  84.1 3.2 %fusion.88 = f32[32,2048]{1,0:T(8,128)} fusion(s32[2048]{0:T(1024)S(1)} %bitcast.177, s32[1024]{0:T(1024)S(1)} %iota_add_fusion.2, f32[32,2048]{1,0:T(8,128)} %get-tuple-element.249, pred[]{:T(512)S(6)} %compare.7, bf16[32,8192]{1,0:T(8,128)(2,1)S(1)} %get-tuple-element.258, s32[]{:T(128)S(6)} %select_n.260), kind=kOutput, calls=%fused_computation.11.clone.1 | convolution fusion | flops 136445952 | bytes 602117 | tf_op jit(solution)/shard_map/while/body/eval_jaxpr/dot_general | solution.py:95
  87.3 3.2 %fusion.88 = f32[32,2048]{1,0:T(8,128)} fusion(s32[2048]{0:T(1024)S(1)} %bitcast.177, s32[1024]{0:T(1024)S(1)} %iota_add_fusion.2, f32[32,2048]{1,0:T(8,128)} %get-tuple-element.249, pred[]{:T(512)S(6)} %compare.7, bf16[32,8192]{1,0:T(8,128)(2,1)S(1)} %get-tuple-element.258, s32[]{:T(128)S(6)} %select_n.260), kind=kOutput, calls=%fused_computation.11.clone.1 | convolution fusion | flops 136445952 | bytes 602117 | tf_op jit(solution)/shard_map/while/body/eval_jaxpr/dot_general | solution.py:95
  90.6 1.0 convert_bitcast_fusion.5
  93.1 1.3 fusion.16
  95.0 3.6 %collective-permute-start.11 = (bf16[2,16,2,256]{3,1,0,2:T(8,128)(2,1)S(1)}, bf16[2,16,2,256]{3,1,0,2:T(8,128)(2,1)S(1)}, u32[]{:S(2)}, u32[]{:S(2)}) collective-permute-start(bf16[2,16,2,256]{3,1,0,2:T(8,128)(2,1)S(1)} %get-tuple-element.179), channel_id=1, source_target_pairs={{0,6},{1,7},{2,4},{3,5},{4,2},{5,3},{6,0},{7,1},{8,14},{9,15},{10,... | collective-permute-start | bytes 98312 | tf_op jit(solution)/shard_map/ppermute | solution.py:205
  98.7 0.8 collective-permute-start.10
  99.4 2.1 %collective-permute-start.12 = (bf16[2,16,2,256]{3,1,0,2:T(8,128)(2,1)S(1)}, bf16[2,16,2,256]{3,1,0,2:T(8,128)(2,1)S(1)}, u32[]{:S(2)}, u32[]{:S(2)}) collective-permute-start(bf16[2,16,2,256]{3,1,0,2:T(8,128)(2,1)S(1)} %get-tuple-element.173), channel_id=1, source_target_pairs={{0,7},{1,6},{2,5},{3,4},{4,3},{5,2},{6,1},{7,0},{8,15},{9,14},{10,... | collective-permute-start | bytes 98312 | tf_op jit(solution)/shard_map/ppermute | solution.py:205
  101.6 1.9 %collective-permute-start.6 = (bf16[2,16,2,256]{3,1,0,2:T(8,128)(2,1)S(1)}, bf16[2,16,2,256]{3,1,0,2:T(8,128)(2,1)S(1)}, u32[]{:S(2)}, u32[]{:S(2)}) collective-permute-start(bf16[2,16,2,256]{3,1,0,2:T(8,128)(2,1)S(1)} %get-tuple-element.175), channel_id=1, source_target_pairs={{0,1},{1,0},{2,3},{3,2},{4,5},{5,4},{6,7},{7,6},{8,9},{9,8},{10,11... | collective-permute-start | bytes 98312 | tf_op jit(solution)/shard_map/ppermute | solution.py:205
  103.4 0.8 collective-permute-start.7
  104.3 1.1 collective-permute-done.6
  105.5 2.2 %collective-permute-start.8 = (bf16[2,16,2,256]{3,1,0,2:T(8,128)(2,1)S(1)}, bf16[2,16,2,256]{3,1,0,2:T(8,128)(2,1)S(1)}, u32[]{:S(2)}, u32[]{:S(2)}) collective-permute-start(bf16[2,16,2,256]{3,1,0,2:T(8,128)(2,1)S(1)} %get-tuple-element.177), channel_id=1, source_target_pairs={{0,3},{1,2},{2,1},{3,0},{4,7},{5,6},{6,5},{7,4},{8,11},{9,10},{10,... | collective-permute-start | bytes 98312 | tf_op jit(solution)/shard_map/ppermute | solution.py:205
  107.6 1.5 collective-permute-start.9
  109.1 1.5 collective-permute-done.8
  110.6 1.9 %collective-permute-done.9 = bf16[2,16,2,256]{3,1,0,2:T(8,128)(2,1)S(1)} collective-permute-done((bf16[2,16,2,256]{3,1,0,2:T(8,128)(2,1)S(1)}, bf16[2,16,2,256]{3,1,0,2:T(8,128)(2,1)S(1)}, u32[]{:S(2)}, u32[]{:S(2)}) %collective-permute-start.9) | collective-permute-done | bytes 32800 | tf_op jit(solution)/shard_map/ppermute | solution.py:205
  113.9 2.8 %collective-permute-start.4 = (bf16[16,16,256]{2,1,0:T(8,128)(2,1)S(1)}, bf16[16,16,256]{2,1,0:T(8,128)(2,1)S(1)}, u32[]{:S(2)}, u32[]{:S(2)}) collective-permute-start(bf16[16,16,256]{2,1,0:T(8,128)(2,1)S(1)} %reshape.177), channel_id=1, source_target_pairs={{0,1},{1,2},{2,3},{3,4},{4,5},{5,6},{6,7},{8,9},{9,10},{10,11},{11... | collective-permute-start | bytes 393224 | tf_op jit(solution)/shard_map/ppermute | solution.py:17
  116.9 1.3 collective-permute-start.5
  118.2 1.0 collective-permute-done.4
  119.3 4.5 %collective-permute-done.5 = bf16[16,16,256]{2,1,0:T(8,128)(2,1)S(1)} collective-permute-done((bf16[16,16,256]{2,1,0:T(8,128)(2,1)S(1)}, bf16[16,16,256]{2,1,0:T(8,128)(2,1)S(1)}, u32[]{:S(2)}, u32[]{:S(2)}) %collective-permute-start.5) | collective-permute-done | bytes 131104 | tf_op jit(solution)/shard_map/ppermute | solution.py:18
  123.8 1.2 gather_fusion.5
  125.0 1.2 gather_fusion.4
  126.8 1.2 gather_fusion.2
  128.0 1.1 fusion.38
  129.1 5.3 %all-gather.2.cloned.1.call-done = bf16[64,16,2,256]{3,1,2,0:T(8,128)(2,1)} async-done(((bf16[16,16,2,256]{3,1,2,0:T(8,128)(2,1)}), bf16[64,16,2,256]{3,1,2,0:T(8,128)(2,1)}) %all-gather.2.cloned.1.call-update) | async-done | bytes 1048592 | tf_op jit(solution)/shard_map/all_gather | solution.py:219
  134.4 3.3 %gather_fusion.1 = bf16[128,16,2,256]{3,1,2,0:T(8,128)(2,1)} fusion(bf16[64,16,2,256]{3,1,2,0:T(8,128)(2,1)} %all-gather.2.cloned.1.call-done, s32[1024]{0:T(1024)S(1)} %pad_clamp_fusion), kind=kCustom, calls=%fused_computation.5 | custom fusion | bytes 4194816 | tf_op jit(solution)/shard_map/jit(_take)/gather | solution.py:220
  137.6 1.9 %select_convert_fusion = f32[16,8,16,2,256]{4,2,3,1,0:T(8,128)S(1)} fusion(bf16[16,8,16,2,256]{4,2,3,1,0:T(8,128)(2,1)} %bitcast.157, pred[16,8]{1,0:T(8,128)(4,1)S(1)} %copy.46), kind=kLoop, calls=%fused_computation.37 | loop fusion | flops 2097152 | bytes 6291584 | tf_op jit(solution)/shard_map/convert_element_type | solution.py:220
  139.6 0.8 subtract_reduce_fusion
  141.1 5.5 %all-to-all-start = ((bf16[16,16,2,256]{3,1,2,0:T(8,128)(2,1)}), bf16[16,16,2,256]{3,1,2,0:T(8,128)(2,1)S(1)}, u32[]{:S(2)}, u32[]{:S(2)}) async-start(bf16[16,16,2,256]{3,1,2,0:T(8,128)(2,1)} %pad_maximum_fusion.8), calls=%async_computation | async-start | bytes 524288 | tf_op jit(solution)/shard_map/all_to_all | solution.py:223
  146.6 1.8 fusion.36
  148.4 1.8 fusion.34
  150.3 5.6 %all-to-all-done = bf16[16,16,2,256]{3,1,2,0:T(8,128)(2,1)S(1)} async-done(((bf16[16,16,2,256]{3,1,2,0:T(8,128)(2,1)}), bf16[16,16,2,256]{3,1,2,0:T(8,128)(2,1)S(1)}, u32[]{:S(2)}, u32[]{:S(2)}) %all-to-all-start) | async-done | bytes 262176 | tf_op jit(solution)/shard_map/all_to_all | solution.py:223
  156.4 4.4 %add_convert_fusion = (bf16[2,8,16,1,2048]{4,3,2,1,0:T(2,128)(2,1)S(1)}, bf16[2,8,16,1,2048]{4,3,2,1,0:T(2,128)(2,1)S(1)}) fusion(f32[2,16,2048]{2,1,0:T(8,128)S(1)} %get-tuple-element.170, f32[8,2048]{1,0:T(8,128)S(1)} %get-tuple-element.186, f32[2,16,2048]{2,1,0:T(8,128)S(1)} %get-tuple-element.169, f32[8,2048]{1,0:T(8,128)S(1)} %get-tuple-element.185), kind=kLoop, calls=%fused_computation.34 | loop fusion | flops 4194304 | bytes 2752512 | tf_op jit(solution)/shard_map/convert.3
  160.8 5.2 %pad_maximum_fusion = bf16[2,8,16,2,2048]{4,3,2,1,0:T(2,128)(2,1)} fusion(bf16[2,8,16,1,2048]{4,3,2,1,0:T(2,128)(2,1)S(1)} %get-tuple-element.168, bf16[2,8,16,1,2048]{4,3,2,1,0:T(2,128)(2,1)S(1)} %get-tuple-element.167), kind=kLoop, calls=%fused_computation.30 | loop fusion | flops 4194304 | bytes 4194304 | tf_op jit(solution)/shard_map/stack | solution.py:76
  166.0 4.1 %convert_element_type.61 = bf16[512,2048]{1,0:T(8,128)(2,1)} reshape(bf16[2,8,16,2,2048]{4,3,2,1,0:T(2,128)(2,1)} %pad_maximum_fusion) | data formatting | bytes 4194304 | tf_op jit(solution)/shard_map/convert_element_type | solution.py:76
  170.2 3.7 %convolution_convert_fusion = bf16[512,512]{1,0:T(8,128)(2,1)} fusion(bf16[512,2048]{1,0:T(8,128)(2,1)} %convert_element_type.61, bf16[512,2048]{1,0:T(8,128)(2,1)S(1)} %copy-done), kind=kOutput, calls=%fused_computation.40 | convolution fusion | flops 1074003968 | bytes 4718592 | tf_op jit(solution)/shard_map/dot_general | solution.py:77
  173.9 2.1 %dot_general.43 = bf16[16,16,1024]{2,1,0:T(8,128)(2,1)} reshape(bf16[512,512]{1,0:T(8,128)(2,1)} %convolution_convert_fusion) | data formatting | bytes 1048576 | tf_op jit(solution)/shard_map/dot_general | solution.py:81
  176.0 1.4 fusion.29
  177.5 1.9 fusion.22
  (134 shorter events, 14.3 us)
Async XLA Ops:
  7.2 85.9 %copy-start = (bf16[512,2048]{1,0:T(8,128)(2,1)S(1)}, bf16[512,2048]{1,0:T(8,128)(2,1)}, u32[]{:S(2)}) copy-start(bf16[512,2048]{1,0:T(8,128)(2,1)} %param.27) | copy-start | bytes 6291460
  7.2 4.7 %copy-start.19 = (s32[4,16,128]{2,1,0:T(8,128)S(1)}, s32[4,16,128]{2,1,0:T(8,128)}, u32[]{:S(2)}) copy-start(s32[4,16,128]{2,1,0:T(8,128)} %param.20) | copy-start | bytes 98308
  7.2 127.2 %all-gather.2.cloned.1.call-start = ((), (), s32[]{:S(2)}) async-start(), calls=%async_computation.1 | async-start | bytes 1310720 | tf_op jit(solution)/shard_map/all_gather | solution.py:219
  7.2 4.6 %copy-start.1 = (f32[2,16,4,16,128]{4,3,2,1,0:T(8,128)S(1)}, f32[2,16,4,16,128]{4,3,2,1,0:T(8,128)}, u32[]{:S(2)}) copy-start(f32[2,16,4,16,128]{4,3,2,1,0:T(8,128)} %param.19) | copy-start | bytes 3145732
  23.3 1.4 copy-start.12
  23.3 5.9 %copy-start.6 = (bf16[2,128,512]{2,1,0:T(8,128)(2,1)S(1)}, bf16[2,128,512]{2,1,0:T(8,128)(2,1)}, u32[]{:S(2)}) copy-start(bf16[2,128,512]{2,1,0:T(8,128)(2,1)} %param.26) | copy-start | bytes 786436
  23.3 7.2 %copy-start.27 = (s32[16,4]{0,1:T(4,128)S(1)}, s32[16,4]{0,1:T(4,128)}, u32[]{:S(2)}) copy-start(s32[16,4]{0,1:T(4,128)} %param.24) | copy-start | bytes 772
  23.3 7.8 %copy-start.23 = (s32[64,8]{0,1:T(8,128)S(1)}, s32[64,8]{0,1:T(8,128)}, u32[]{:S(2)}) copy-start(s32[64,8]{0,1:T(8,128)} %param.29) | copy-start | bytes 6148
  23.3 7.8 %copy-start.24 = (s32[64,8]{0,1:T(8,128)S(1)}, s32[64,8]{0,1:T(8,128)}, u32[]{:S(2)}) copy-start(s32[64,8]{0,1:T(8,128)} %param.30) | copy-start | bytes 6148
  24.6 8.3 %collective-permute-start = (bf16[66,2,16,128]{3,2,1,0:T(8,128)(2,1)}, bf16[66,2,16,128]{3,2,1,0:T(8,128)(2,1)}, u32[]{:S(2)}, u32[]{:S(2)}) collective-permute-start(bf16[66,2,16,128]{3,2,1,0:T(8,128)(2,1)} %get-tuple-element.165), channel_id=1, source_target_pairs={{0,8},{8,16},{16,24},{1,9},{9,17},{17,25},{2,10},{10,18},{18,26},{... | collective-permute-start | bytes 1622024 | tf_op jit(solution)/shard_map/ppermute | solution.py:17
  27.9 5.5 %collective-permute-start.1 = (bf16[66,2,16,128]{3,2,1,0:T(8,128)(2,1)}, bf16[66,2,16,128]{3,2,1,0:T(8,128)(2,1)}, u32[]{:S(2)}, u32[]{:S(2)}) collective-permute-start(bf16[66,2,16,128]{3,2,1,0:T(8,128)(2,1)} %get-tuple-element.166), channel_id=1, source_target_pairs={{8,0},{16,8},{24,16},{9,1},{17,9},{25,17},{10,2},{18,10},{26,18},{... | collective-permute-start | bytes 1622024 | tf_op jit(solution)/shard_map/ppermute | solution.py:18
  37.8 11.8 %collective-permute-start.2 = (bf16[66,8,2,128]{3,2,1,0:T(2,128)(2,1)}, bf16[66,8,2,128]{3,2,1,0:T(2,128)(2,1)}, u32[]{:S(2)}, u32[]{:S(2)}) collective-permute-start(bf16[66,8,2,128]{3,2,1,0:T(2,128)(2,1)} %get-tuple-element.163), channel_id=1, source_target_pairs={{0,1},{1,2},{2,3},{3,4},{4,5},{5,6},{6,7},{8,9},{9,10},{10,11},{11... | collective-permute-start | bytes 811016 | tf_op jit(solution)/shard_map/ppermute | solution.py:17
  42.4 8.7 %collective-permute-start.3 = (bf16[66,8,2,128]{3,2,1,0:T(2,128)(2,1)}, bf16[66,8,2,128]{3,2,1,0:T(2,128)(2,1)}, u32[]{:S(2)}, u32[]{:S(2)}) collective-permute-start(bf16[66,8,2,128]{3,2,1,0:T(2,128)(2,1)} %get-tuple-element.164), channel_id=1, source_target_pairs={{1,0},{2,1},{3,2},{4,3},{5,4},{6,5},{7,6},{9,8},{10,9},{11,10},{12... | collective-permute-start | bytes 811016 | tf_op jit(solution)/shard_map/ppermute | solution.py:18
  49.6 8.5 %copy-start.20 = (pred[6,18]{1,0:T(8,128)(4,1)S(1)}, pred[6,18]{1,0:T(8,128)(4,1)}, u32[]{:S(2)}) copy-start(pred[6,18]{1,0:T(8,128)(4,1)} %broadcast_and_fusion) | copy-start | bytes 328
  62.4 0.8 copy-start.11
  62.4 0.8 copy-start.13
  62.9 1.2 copy-start.2
  64.2 1.6 copy-start.28
  65.8 26.6 %copy-start.14 = (bf16[128,512]{1,0:T(8,128)(2,1)S(1)}, bf16[128,512]{1,0:T(8,128)(2,1)}, u32[]{:S(2)}) copy-start(bf16[128,512]{1,0:T(8,128)(2,1)} %fusion.71) | copy-start | bytes 393220
  65.8 26.6 %copy-start.16 = (bf16[128,512]{1,0:T(8,128)(2,1)S(1)}, bf16[128,512]{1,0:T(8,128)(2,1)}, u32[]{:S(2)}) copy-start(bf16[128,512]{1,0:T(8,128)(2,1)} %get-tuple-element.181) | copy-start | bytes 393220
  65.8 26.6 %copy-start.18 = (bf16[128,512]{1,0:T(8,128)(2,1)S(1)}, bf16[128,512]{1,0:T(8,128)(2,1)}, u32[]{:S(2)}) copy-start(bf16[128,512]{1,0:T(8,128)(2,1)} %get-tuple-element.182) | copy-start | bytes 393220
  91.7 0.7 copy-start.9
  94.3 19.0 %copy-start.22 = (s32[16,4]{0,1:T(4,128)S(1)}, s32[16,4]{0,1:T(4,128)}, u32[]{:S(2)}) copy-start(s32[16,4]{0,1:T(4,128)} %broadcast_subtract_fusion) | copy-start | bytes 772
  94.3 19.1 %copy-start.21 = (pred[16,8]{1,0:T(8,128)(4,1)S(1)}, pred[16,8]{1,0:T(8,128)(4,1)}, u32[]{:S(2)}) copy-start(pred[16,8]{1,0:T(8,128)(4,1)} %copy.44) | copy-start | bytes 388
  95.0 18.8 %copy-start.10 = (bf16[2,16,16,128]{3,0,1,2:T(2,128)(2,1)S(1)}, bf16[2,16,16,128]{3,0,1,2:T(2,128)(2,1)}, u32[]{:S(2)}) copy-start(bf16[2,16,16,128]{3,0,1,2:T(2,128)(2,1)} %copy-done.9) | copy-start | bytes 393220
  95.0 21.7 %copy-start.26 = (s32[128]{0:T(128)S(1)}, s32[128]{0:T(128)}, u32[]{:S(2)}) copy-start(s32[128]{0:T(128)} %reshape.222) | copy-start | bytes 1540
  95.0 21.8 %copy-start.25 = (pred[16,8]{0,1:T(8,128)(4,1)S(1)}, pred[16,8]{0,1:T(8,128)(4,1)}, u32[]{:S(2)}) copy-start(pred[16,8]{0,1:T(8,128)(4,1)} %get-tuple-element.137) | copy-start | bytes 388
  95.0 17.5 %collective-permute-start.11 = (bf16[2,16,2,256]{3,1,0,2:T(8,128)(2,1)S(1)}, bf16[2,16,2,256]{3,1,0,2:T(8,128)(2,1)S(1)}, u32[]{:S(2)}, u32[]{:S(2)}) collective-permute-start(bf16[2,16,2,256]{3,1,0,2:T(8,128)(2,1)S(1)} %get-tuple-element.179), channel_id=1, source_target_pairs={{0,6},{1,7},{2,4},{3,5},{4,2},{5,3},{6,0},{7,1},{8,14},{9,15},{10,... | collective-permute-start | bytes 98312 | tf_op jit(solution)/shard_map/ppermute | solution.py:205
  98.7 13.9 %collective-permute-start.10 = (bf16[2,16,2,256]{3,1,0,2:T(8,128)(2,1)S(1)}, bf16[2,16,2,256]{3,1,0,2:T(8,128)(2,1)S(1)}, u32[]{:S(2)}, u32[]{:S(2)}) collective-permute-start(bf16[2,16,2,256]{3,1,0,2:T(8,128)(2,1)S(1)} %get-tuple-element.180), channel_id=1, source_target_pairs={{0,5},{1,4},{2,7},{3,6},{4,1},{5,0},{6,3},{7,2},{8,13},{9,12},{10,... | collective-permute-start | bytes 98312 | tf_op jit(solution)/shard_map/ppermute | solution.py:205
  99.4 13.1 %collective-permute-start.12 = (bf16[2,16,2,256]{3,1,0,2:T(8,128)(2,1)S(1)}, bf16[2,16,2,256]{3,1,0,2:T(8,128)(2,1)S(1)}, u32[]{:S(2)}, u32[]{:S(2)}) collective-permute-start(bf16[2,16,2,256]{3,1,0,2:T(8,128)(2,1)S(1)} %get-tuple-element.173), channel_id=1, source_target_pairs={{0,7},{1,6},{2,5},{3,4},{4,3},{5,2},{6,1},{7,0},{8,15},{9,14},{10,... | collective-permute-start | bytes 98312 | tf_op jit(solution)/shard_map/ppermute | solution.py:205
  101.6 3.9 %collective-permute-start.6 = (bf16[2,16,2,256]{3,1,0,2:T(8,128)(2,1)S(1)}, bf16[2,16,2,256]{3,1,0,2:T(8,128)(2,1)S(1)}, u32[]{:S(2)}, u32[]{:S(2)}) collective-permute-start(bf16[2,16,2,256]{3,1,0,2:T(8,128)(2,1)S(1)} %get-tuple-element.175), channel_id=1, source_target_pairs={{0,1},{1,0},{2,3},{3,2},{4,5},{5,4},{6,7},{7,6},{8,9},{9,8},{10,11... | collective-permute-start | bytes 98312 | tf_op jit(solution)/shard_map/ppermute | solution.py:205
  103.4 4.2 %collective-permute-start.7 = (bf16[2,16,2,256]{3,1,0,2:T(8,128)(2,1)S(1)}, bf16[2,16,2,256]{3,1,0,2:T(8,128)(2,1)S(1)}, u32[]{:S(2)}, u32[]{:S(2)}) collective-permute-start(bf16[2,16,2,256]{3,1,0,2:T(8,128)(2,1)S(1)} %get-tuple-element.176), channel_id=1, source_target_pairs={{0,2},{1,3},{2,0},{3,1},{4,6},{5,7},{6,4},{7,5},{8,10},{9,11},{10,... | collective-permute-start | bytes 98312 | tf_op jit(solution)/shard_map/ppermute | solution.py:205
  105.5 5.2 %collective-permute-start.8 = (bf16[2,16,2,256]{3,1,0,2:T(8,128)(2,1)S(1)}, bf16[2,16,2,256]{3,1,0,2:T(8,128)(2,1)S(1)}, u32[]{:S(2)}, u32[]{:S(2)}) collective-permute-start(bf16[2,16,2,256]{3,1,0,2:T(8,128)(2,1)S(1)} %get-tuple-element.177), channel_id=1, source_target_pairs={{0,3},{1,2},{2,1},{3,0},{4,7},{5,6},{6,5},{7,4},{8,11},{9,10},{10,... | collective-permute-start | bytes 98312 | tf_op jit(solution)/shard_map/ppermute | solution.py:205
  107.6 4.9 %collective-permute-start.9 = (bf16[2,16,2,256]{3,1,0,2:T(8,128)(2,1)S(1)}, bf16[2,16,2,256]{3,1,0,2:T(8,128)(2,1)S(1)}, u32[]{:S(2)}, u32[]{:S(2)}) collective-permute-start(bf16[2,16,2,256]{3,1,0,2:T(8,128)(2,1)S(1)} %get-tuple-element.178), channel_id=1, source_target_pairs={{0,4},{1,5},{2,6},{3,7},{4,0},{5,1},{6,2},{7,3},{8,12},{9,13},{10,... | collective-permute-start | bytes 98312 | tf_op jit(solution)/shard_map/ppermute | solution.py:205
  112.6 0.7 copy-start.3
  113.9 5.3 %collective-permute-start.4 = (bf16[16,16,256]{2,1,0:T(8,128)(2,1)S(1)}, bf16[16,16,256]{2,1,0:T(8,128)(2,1)S(1)}, u32[]{:S(2)}, u32[]{:S(2)}) collective-permute-start(bf16[16,16,256]{2,1,0:T(8,128)(2,1)S(1)} %reshape.177), channel_id=1, source_target_pairs={{0,1},{1,2},{2,3},{3,4},{4,5},{5,6},{6,7},{8,9},{9,10},{10,11},{11... | collective-permute-start | bytes 393224 | tf_op jit(solution)/shard_map/ppermute | solution.py:17
  116.9 6.9 %collective-permute-start.5 = (bf16[16,16,256]{2,1,0:T(8,128)(2,1)S(1)}, bf16[16,16,256]{2,1,0:T(8,128)(2,1)S(1)}, u32[]{:S(2)}, u32[]{:S(2)}) collective-permute-start(bf16[16,16,256]{2,1,0:T(8,128)(2,1)S(1)} %reshape.177), channel_id=1, source_target_pairs={{1,0},{2,1},{3,2},{4,3},{5,4},{6,5},{7,6},{9,8},{10,9},{11,10},{12... | collective-permute-start | bytes 393224 | tf_op jit(solution)/shard_map/ppermute | solution.py:18
  139.6 7.0 %copy-start.7 = (bf16[4,256,256]{2,1,0:T(8,128)(2,1)S(1)}, bf16[4,256,256]{2,1,0:T(8,128)(2,1)}, u32[]{:S(2)}) copy-start(bf16[4,256,256]{2,1,0:T(8,128)(2,1)} %param.25) | copy-start | bytes 1572868
  141.1 14.8 %all-to-all-start = ((bf16[16,16,2,256]{3,1,2,0:T(8,128)(2,1)}), bf16[16,16,2,256]{3,1,2,0:T(8,128)(2,1)S(1)}, u32[]{:S(2)}, u32[]{:S(2)}) async-start(bf16[16,16,2,256]{3,1,2,0:T(8,128)(2,1)} %pad_maximum_fusion.8), calls=%async_computation | async-start | bytes 524288 | tf_op jit(solution)/shard_map/all_to_all | solution.py:223
  170.2 5.8 %copy-start.15 = (bf16[128,512]{1,0:T(8,128)(2,1)S(1)}, bf16[128,512]{1,0:T(8,128)(2,1)}, u32[]{:S(2)}) copy-start(bf16[128,512]{1,0:T(8,128)(2,1)} %fusion.71) | copy-start | bytes 393220
  170.2 5.8 %copy-start.17 = (bf16[128,512]{1,0:T(8,128)(2,1)S(1)}, bf16[128,512]{1,0:T(8,128)(2,1)}, u32[]{:S(2)}) copy-start(bf16[128,512]{1,0:T(8,128)(2,1)} %get-tuple-element.181) | copy-start | bytes 393220
  173.9 3.6 %copy-start.4 = (f32[16,16,256]{2,1,0:T(8,128)S(1)}, f32[16,16,256]{2,1,0:T(8,128)}, u32[]{:S(2)}) copy-start(f32[16,16,256]{2,1,0:T(8,128)} %fusion.36) | copy-start | bytes 786436
  173.9 3.6 %copy-start.5 = (f32[16,16,256]{2,1,0:T(8,128)S(1)}, f32[16,16,256]{2,1,0:T(8,128)}, u32[]{:S(2)}) copy-start(f32[16,16,256]{2,1,0:T(8,128)} %fusion.34) | copy-start | bytes 786436
  173.9 3.6 %copy-start.8 = (bf16[16,16,256]{2,1,0:T(8,128)(2,1)S(1)}, bf16[16,16,256]{2,1,0:T(8,128)(2,1)}, u32[]{:S(2)}) copy-start(bf16[16,16,256]{2,1,0:T(8,128)(2,1)} %gather_fusion.2) | copy-start | bytes 393220
Sparse Core Ops, SparseCore 0:
  113.5 20.8 all-gather.1
